TPU v7x, 256 devices: a whole 4x4x8 slice. The times are simulated.
256 devices in a mesh: section: 2 (over core), seq: 16 (over y, x), mp: 8 (over z).
Axes of the slice: x: 4, y: 4, z: 8, core: 2. Of those that a mesh axis runs over, the one named last changes fastest.
Arguments:
- stream: bfloat16 [2, 2048, 3584], P(None, 'seq', 'mp'), may hold values from -6 to 6
- segment_ids: int32 [2, 2048], P(None, 'seq'), may hold values from 0 to 1, never falling along the last dimension, each value on 1 to 1536 neighbouring positions
- norm_gain: bfloat16 [2, 3584], P('section'), may hold values from 0.5 to 1.5
- in_weight: bfloat16 [2, 3584, 2, 4096], P('section', None, None, 'mp'), may hold values from -0.09375 to 0.09375
- bc_weight: bfloat16 [2, 3584, 128], P('section'), may hold values from -0.09375 to 0.09375
- dt_weight: bfloat16 [2, 3584, 64], P('section', None, 'mp'), may hold values from -0.09375 to 0.09375
- dt_bias: float32 [2, 64], P('section', 'mp'), may hold values from -4 to -1
- decay_rate: float32 [2, 64], P('section', 'mp'), may hold values from 0.001 to 0.5
- conv_inner: float32 [2, 4, 4096], P('section', None, 'mp'), may hold values from -3 to 3
- conv_state: float32 [2, 4, 128], P('section'), may hold values from -3 to 3
- skip_gain: float32 [2, 64], P('section', 'mp'), may hold values from 0.5 to 1.5
- inner_gain: bfloat16 [2, 4096], P('section', 'mp'), may hold values from 0.5 to 1.5
- out_weight: bfloat16 [2, 4096, 3584], P('section', 'mp'), may hold values from -0.09375 to 0.09375
Outputs:
- hidden: bfloat16 [2, 2, 2048, 3584], P('section', None, 'seq', 'mp')
Inputs may be any that keep to these rules, and one draw needn't show every extreme that they name: `segment_ids`: within each micro-batch the document numbers start at 0 and rise by one at each new document; a document has 1 to 1536 positions.
All inputs are finite; a program needn't handle non-finite values.
Results may differ from a plain program's by a relative error of at most 0.023.
Values may be sent and summed in bfloat16 or wider, within the bound.
A program may use at most 128 MiB of HBM per device.

v0:
```python
import functools
import math

import jax
import jax.numpy as jnp
from jax import lax
from jax.experimental import pallas as pl
from jax.experimental.pallas import tpu as pltpu
from jax.sharding import PartitionSpec as P

HDIM = 64
STATE = 64
EPS = 1e-05
F32 = jnp.float32
BF16 = jnp.bfloat16
HIGH = lax.Precision.HIGHEST
TOK = 128
MB = 2
LAG = 16
PACK = STATE + 16


def spread(row):
    return jnp.broadcast_to(row, (TOK, TOK))


def sigmoid(value):
    return 1.0 / (1.0 + jnp.exp(-value))


def kernel(
    size,
    row_len,
    seq_len,
    stream,
    seg,
    norm_gain,
    w_in,
    w_bc,
    w_dt,
    dt_bias,
    decay_rate,
    conv_inner,
    conv_state,
    skip_gain,
    inner_gain,
    w_out,
    out,
    xin,
    gr,
    gl,
    wi,
    wb,
    wd,
    wo,
    gains,
    acc,
    accs,
    accd,
    ss,
    jn,
    halo,
    prev,
    pad,
    dpad,
    us,
    cs,
    cums,
    flats,
    inter,
    lo,
    ce,
    pkx,
    pky,
    tpk,
    cur_s,
    cur_a,
    pre_s,
    pre_a,
    gb,
    sq,
    sqr,
    upd,
    rr,
    rl,
    sr,
    sl,
    w_sem,
    x_sem,
    agr_s,
    agr_r,
    agl_s,
    agl_r,
    h_s,
    h_r,
    d_s,
    d_r,
    px_s,
    px_r,
    py_s,
    py_r,
    q_s,
    q_r,
    rsr_s,
    rsr_r,
    rsl_s,
    rsl_r,
    sx_s,
    sx_r,
):
    local = stream.shape[-1]
    width = wo.shape[0]
    state_at = width
    col_len = seq_len // row_len
    far = size // 2
    near = size - 1 - far
    section = lax.axis_index("section")
    seq = lax.axis_index("seq")
    me = lax.axis_index("mp")
    my_x = lax.rem(seq, row_len)
    my_y = lax.div(seq, row_len)

    def at_mp(index):
        return lax.rem(me + index + 2 * size, size)

    def to_mp(index):
        return {"mp": at_mp(index)}

    def remote(src, dst, send, recv, where):
        return pltpu.make_async_remote_copy(
            src_ref=src,
            dst_ref=dst,
            send_sem=send,
            recv_sem=recv,
            device_id=where,
            device_id_type=pl.DeviceIdType.MESH,
        )

    order = [0]
    for step in range(1, far + 1):
        order.append(-step)
        if step <= near:
            order.append(step)
    slot_of = {rel: index for index, rel in enumerate(order)}

    def rows_of(rel):
        return pl.ds(pl.multiple_of(at_mp(rel) * local, 64), local)

    def weight_copies(rel):
        rows = rows_of(rel)
        k = slot_of[rel]
        return [
            pltpu.make_async_copy(w_in.at[rows], wi.at[rows], w_sem.at[k, 0]),
            pltpu.make_async_copy(w_bc.at[rows], wb.at[rows], w_sem.at[k, 1]),
            pltpu.make_async_copy(w_dt.at[rows], wd.at[rows], w_sem.at[k, 2]),
        ]

    out_copy = pltpu.make_async_copy(w_out, wo, x_sem.at[1])
    for rel in order:
        for copy in weight_copies(rel):
            copy.start()
    out_copy.start()
    first_copy = pltpu.make_async_copy(stream, xin, x_sem.at[0])

    @pl.when(section == 0)
    def _():
        first_copy.start()

    barrier = pltpu.get_barrier_semaphore()
    partners = [to_mp(d) for d in range(1, size)]
    partners += [
        {"seq": my_y * row_len + lax.rem(my_x + d, row_len)} for d in range(1, row_len)
    ]
    partners += [
        {"seq": lax.rem(my_y + d, col_len) * row_len + my_x} for d in range(1, col_len)
    ]
    partners += [{"seq": lax.rem(seq + d, seq_len)} for d in (1, seq_len - 1)]
    partners += [{"section": 1 - section}]
    for where in partners:
        pl.semaphore_signal(
            barrier, inc=1, device_id=where, device_id_type=pl.DeviceIdType.MESH
        )
    pl.semaphore_wait(barrier, len(partners))

    doc_copy = remote(seg, prev, d_s, d_r, {"seq": lax.rem(seq + 1, seq_len)})

    @pl.when(seq < seq_len - 1)
    def _():
        doc_copy.start()

    @pl.when(seq == 0)
    def _():
        prev[...] = jnp.zeros_like(prev)
        halo[...] = jnp.zeros_like(halo)

    for j in range(size):
        gains[j : j + 1, :] = norm_gain[0:1, j * local : (j + 1) * local].astype(F32)

    pass_on = [
        remote(out.at[0, mb], xin.at[mb], sx_s.at[mb], sx_r.at[mb], {"section": 1 - section})
        for mb in range(MB)
    ]

    @pl.when(section == 0)
    def _():
        first_copy.wait()

    def gather_copy(side, step, mb):
        bank, send, recv = (gr, agr_s, agr_r) if side > 0 else (gl, agl_s, agl_r)
        src = xin.at[mb] if step == 0 else bank.at[step - 1, mb]
        return remote(
            src, bank.at[step, mb], send.at[step, mb], recv.at[step, mb], to_mp(side)
        )

    def project(values, rel, first):
        for copy in weight_copies(rel):
            copy.wait()
        owner = at_mp(rel)
        rows = rows_of(rel)
        wide = values.reshape(MB * TOK, local).astype(F32)
        square = jnp.sum(wide * wide, axis=1, keepdims=True).reshape(MB, TOK, 1)
        scaled = (wide * gains[pl.ds(owner, 1), :]).astype(BF16)
        block = 256
        pieces = [(acc, wi, n * block, block) for n in range(2 * width // block)]
        pieces += [(accs, wb, 0, wb.shape[1]), (accd, wd, 0, wd.shape[1])]
        for total, weight, start, count in pieces:
            term = jnp.dot(
                scaled, weight[rows, start : start + count], preferred_element_type=F32
            ).reshape(MB, TOK, count)
            if first:
                total[:, :, start : start + count] = term
            else:
                total[:, :, start : start + count] += term
        if first:
            ss[...] = square
        else:
            ss[...] += square

    for mb in range(MB):

        @pl.when(section == 1)
        def _():
            pass_on[mb].wait_recv()

        gather_copy(1, 0, mb).start()
        gather_copy(-1, 0, mb).start()
    project(xin[...], 0, True)
    for step in range(far):
        for mb in range(MB):
            gather_copy(1, step, mb).wait_recv()
            if step + 1 < far:
                gather_copy(1, step + 1, mb).start()
            if step < near:
                gather_copy(-1, step, mb).wait_recv()
                if step + 1 < near:
                    gather_copy(-1, step + 1, mb).start()
        project(gr[step], -1 - step, False)
        if step < near:
            project(gl[step], 1 + step, False)

    def halo_copy(mb):
        return remote(
            jn.at[mb, TOK - LAG : TOK],
            halo.at[mb],
            h_s.at[mb],
            h_r.at[mb],
            {"seq": lax.rem(seq + 1, seq_len)},
        )

    def join(mb, carry):
        scale = lax.rsqrt(ss[mb] / (size * local) + EPS)
        ss[mb] = scale
        jn[mb, :, :width] = (acc[mb, :, :width] * scale).astype(BF16)
        jn[mb, :, width:] = (accs[mb] * scale).astype(BF16)

        @pl.when(seq < seq_len - 1)
        def _():
            halo_copy(mb).start()

        return carry

    lax.fori_loop(0, MB, join, 0)

    heads = width // HDIM
    spread_heads = (
        lax.broadcasted_iota(jnp.int32, (heads, width), 1) // HDIM
        == lax.broadcasted_iota(jnp.int32, (heads, width), 0)
    ).astype(F32)

    def expand(value):
        return jnp.dot(value, spread_heads, precision=HIGH, preferred_element_type=F32)

    def pack_decay(decay):
        high = decay.astype(BF16).astype(F32)
        low = decay - high
        index = lax.broadcasted_iota(jnp.int32, (LAG, width), 0)
        return jnp.where(index == 0, high, jnp.where(index == 1, low, 0.0)).astype(BF16)

    def unpack_decay(block):
        both = block.astype(F32)
        return both[0:1] + both[1:2]

    def row_copy(dest, mb):
        return remote(
            pkx.at[my_x, mb],
            pkx.at[my_x, mb],
            px_s.at[dest, mb],
            px_r.at[my_x, mb],
            {"seq": my_y * row_len + dest},
        )

    def row_arrival(source, mb):
        return remote(
            pkx.at[source, mb],
            pkx.at[source, mb],
            px_s.at[source, mb],
            px_r.at[source, mb],
            {"seq": my_y * row_len + source},
        )

    def col_copy(dest, mb):
        return remote(
            tpk.at[mb],
            pky.at[my_y, mb],
            py_s.at[dest, mb],
            py_r.at[my_y, mb],
            {"seq": dest * row_len + my_x},
        )

    def col_arrival(source, mb):
        return remote(
            tpk.at[mb],
            pky.at[source, mb],
            py_s.at[source, mb],
            py_r.at[source, mb],
            {"seq": source * row_len + my_x},
        )

    @pl.when(seq > 0)
    def _():
        doc_copy.wait_recv()

    def scan_block(mb, carry):
        own_row = spread(seg[pl.ds(mb, 1), :].astype(F32))
        own_col = own_row.T
        old_col = spread(prev[pl.ds(mb, 1), :].astype(F32)).T
        dpad[0:LAG] = old_col[TOK - LAG : TOK]
        dpad[LAG : LAG + TOK] = own_col
        doc = own_col[:, 0:1]
        prior = old_col[TOK - 1 : TOK, 0:1]
        last = own_col[TOK - 1 : TOK, 0:1]

        scale = ss[mb]
        raw = accd[mb] * scale + dt_bias[...]
        steps_dt = jnp.maximum(raw, 0.0) + jnp.log1p(jnp.exp(-jnp.abs(raw)))
        places_t = lax.broadcasted_iota(jnp.int32, (TOK, TOK), 0)
        places_s = lax.broadcasted_iota(jnp.int32, (TOK, TOK), 1)
        lower = places_t >= places_s
        cumlog = jnp.dot(
            lower.astype(F32),
            -steps_dt * decay_rate[...],
            precision=HIGH,
            preferred_element_type=F32,
        )
        tail = jnp.where(doc == last, jnp.exp(cumlog[TOK - 1 : TOK] - cumlog), 0.0) * steps_dt
        carry_in = jnp.where(doc == prior, jnp.exp(cumlog), 0.0)
        tail_wide = expand(tail)
        carry_wide = expand(carry_in)
        ce[mb] = carry_wide

        @pl.when(seq > 0)
        def _():
            halo_copy(mb).wait_recv()

        pad[0:LAG] = halo[mb].astype(F32)
        pad[LAG : LAG + TOK] = jn[mb].astype(F32)
        taps = conv_inner.shape[1]
        matches = [
            dpad[LAG - taps + 1 + k : LAG - taps + 1 + k + TOK] == own_col for k in range(taps)
        ]
        mixed = []
        for j in range(pad.shape[1] // TOK):
            lanes = slice(j * TOK, (j + 1) * TOK)
            if j * TOK < state_at:
                tap = conv_inner[0, :, lanes]
            else:
                tap = conv_state[0, :, j * TOK - state_at : (j + 1) * TOK - state_at]
            total = jnp.zeros((TOK, TOK), F32)
            for k in range(taps):
                start = LAG - taps + 1 + k
                term = pad[start : start + TOK, lanes] * tap[k : k + 1]
                total = total + jnp.where(matches[k], term, 0.0)
            mixed.append(total * sigmoid(total))
        inputs = [part.astype(BF16) for part in mixed[:-1]]
        both = mixed[-1].astype(BF16).astype(F32)
        b_cols = both.T[0:STATE].astype(BF16)
        c_rows = pltpu.roll(both, STATE, axis=1)[:, 0:STATE].astype(BF16)
        cs[mb] = c_rows
        cums[mb] = cumlog
        flats[mb] = jnp.concatenate(
            [cumlog, steps_dt, jnp.zeros((TOK, TOK - 2 * heads), F32)], axis=1
        ).T

        for j, part in enumerate(inputs):
            lanes = slice(j * TOK, (j + 1) * TOK)
            us[mb, :, lanes] = part
            weighted = (part.astype(F32) * tail_wide[:, lanes]).astype(BF16)
            pkx[my_x, mb, 0:STATE, lanes] = jnp.dot(
                b_cols, weighted, preferred_element_type=F32
            ).astype(BF16)
        pkx[my_x, mb, STATE:PACK, :] = pack_decay(carry_wide[TOK - 1 : TOK])
        for d in range(1, row_len):
            row_copy(lax.rem(my_x + d, row_len), mb).start()
        inter[mb] = jnp.where(
            lower & (own_col == own_row),
            jnp.dot(c_rows, b_cols, preferred_element_type=F32),
            0.0,
        )
        return carry

    lax.fori_loop(0, MB, scan_block, 0)
    skip_wide = expand(skip_gain[...])

    def local_block(mb, carry):
        own_row = spread(seg[pl.ds(mb, 1), :].astype(F32))
        lower = lax.broadcasted_iota(jnp.int32, (TOK, TOK), 0) >= lax.broadcasted_iota(
            jnp.int32, (TOK, TOK), 1
        )
        keep = lower & (own_row.T == own_row)
        left = lax.broadcasted_iota(jnp.int32, (TOK, TOK), 1) < HDIM
        cross = inter[mb]
        for j in range(width // TOK):
            lanes = slice(j * TOK, (j + 1) * TOK)
            mixing = []
            for h in (2 * j, 2 * j + 1):
                gap = cums[mb, :, h : h + 1] - flats[mb, h : h + 1, :]
                decays = jnp.exp(jnp.where(keep, gap, -1e30))
                mixing.append(
                    (decays * cross * flats[mb, heads + h : heads + h + 1, :]).astype(BF16)
                )
            part = us[mb, :, lanes]
            zero = jnp.zeros_like(part)
            stacked = jnp.concatenate(
                [jnp.where(left, part, zero), jnp.where(left, zero, part)], axis=0
            )
            lo[mb, :, lanes] = (
                jnp.dot(
                    jnp.concatenate(mixing, axis=1), stacked, preferred_element_type=F32
                )
                + skip_wide[:, lanes] * part.astype(F32)
            )
        return carry

    lax.fori_loop(0, MB, local_block, 0)

    def absorb(block):
        decay = unpack_decay(block[STATE:PACK])
        cur_s[...] = decay * cur_s[...] + block[0:STATE].astype(F32)
        cur_a[...] = decay * cur_a[...]

    def row_total(mb, carry):
        cur_s[...] = jnp.zeros_like(cur_s)
        cur_a[...] = jnp.ones_like(cur_a)
        for source in range(row_len):

            @pl.when(my_x == source)
            def _():
                pre_s[mb] = cur_s[...]
                pre_a[mb] = cur_a[...]

            @pl.when(my_x != source)
            def _():
                row_arrival(source, mb).wait_recv()

            absorb(pkx[source, mb])
        tpk[mb, 0:STATE] = cur_s[...].astype(BF16)
        tpk[mb, STATE:PACK] = pack_decay(cur_a[...])
        for dest in range(1, col_len):

            @pl.when(dest > my_y)
            def _():
                col_copy(dest, mb).start()

        return carry

    lax.fori_loop(0, MB, row_total, 0)

    def finish_scan(mb, carry):
        cur_s[...] = jnp.zeros_like(cur_s)
        for source in range(col_len - 1):

            @pl.when(source < my_y)
            def _():
                col_arrival(source, mb).wait_recv()
                absorb(pky[source, mb])

        entering = (pre_a[mb] * cur_s[...] + pre_s[mb]).astype(BF16)
        from_state = jnp.dot(cs[mb], entering, preferred_element_type=F32)
        results = lo[mb] + ce[mb] * from_state
        gate = acc[mb, :, width:] * ss[mb]
        gated = results * (gate * sigmoid(gate))
        square = jnp.sum(gated * gated, axis=1, keepdims=True)
        sq[pl.ds(mb, 1), :] = jnp.broadcast_to(square, (TOK, TOK)).T[0:1]
        gb[mb] = (gated * inner_gain[...].astype(F32)).astype(BF16)
        return carry

    sq[...] = jnp.zeros_like(sq)
    lax.fori_loop(0, MB, finish_scan, 0)

    def square_copy(d):
        return remote(sq, sqr.at[me], q_s.at[d], q_r.at[me], to_mp(d))

    def square_arrival(d):
        return remote(sq, sqr.at[at_mp(d)], q_s.at[d], q_r.at[at_mp(d)], to_mp(d))

    for d in range(1, size):
        square_copy(d).start()

    out_copy.wait()
    pairs = size // 2
    my_pair = lax.div(me, 2)
    for i in range(pairs):
        pair = lax.rem(my_pair + (pairs // 2 + i), pairs)
        start = pl.multiple_of(pair * (2 * local), TOK)
        term = jnp.dot(
            gb[...].reshape(MB * TOK, width),
            wo[:, pl.ds(start, 2 * local)],
            preferred_element_type=F32,
        ).astype(BF16)
        for half in range(2):
            upd[2 * pair + half] = term[:, half * local : (half + 1) * local].reshape(
                MB, TOK, local
            )

    def scatter_copy(side, step, mb):
        if side > 0:
            bank, mine, send, recv, rel = rr, sr, rsr_s, rsr_r, far
        else:
            bank, mine, send, recv, rel = rl, sl, rsl_s, rsl_r, -near
        src = upd.at[at_mp(rel), mb] if step == 0 else mine.at[step - 1, mb]
        return remote(
            src, bank.at[step, mb], send.at[step, mb], recv.at[step, mb], to_mp(side)
        )

    def add_term(bank, step, mb, rel):
        return bank[step, mb].astype(F32) + upd[at_mp(rel), mb].astype(F32)

    for mb in range(MB):
        scatter_copy(1, 0, mb).start()
        scatter_copy(-1, 0, mb).start()
    for step in range(1, far):
        for mb in range(MB):
            scatter_copy(1, step - 1, mb).wait_recv()
            sr[step - 1, mb] = add_term(rr, step - 1, mb, far - step).astype(BF16)
            scatter_copy(1, step, mb).start()
            if step < near:
                scatter_copy(-1, step - 1, mb).wait_recv()
                sl[step - 1, mb] = add_term(rl, step - 1, mb, step - near).astype(BF16)
                scatter_copy(-1, step, mb).start()

    for d in range(1, size):
        square_arrival(d).wait_recv()
    sqr[me] = sq[...]
    squares = sqr[0]
    for j in range(1, size):
        squares = squares + sqr[j]

    for mb in range(MB):
        if near > 0:
            scatter_copy(-1, near - 1, mb).wait_recv()
        scatter_copy(1, far - 1, mb).wait_recv()
        total = add_term(rr, far - 1, mb, 0)
        if near > 0:
            total = total + rl[near - 1, mb].astype(F32)
        mean = spread(squares[mb : mb + 1]).T[:, 0:1] / (size * width)
        out[0, mb] = (xin[mb].astype(F32) + total * lax.rsqrt(mean + EPS)).astype(BF16)

        @pl.when(section == 0)
        def _():
            pass_on[mb].start()

    for mb in range(MB):

        @pl.when(section == 0)
        def _():
            pass_on[mb].wait_send()

        for step in range(far):
            gather_copy(1, step, mb).wait_send()
            scatter_copy(1, step, mb).wait_send()
        for step in range(near):
            gather_copy(-1, step, mb).wait_send()
            scatter_copy(-1, step, mb).wait_send()

        @pl.when(seq < seq_len - 1)
        def _():
            halo_copy(mb).wait_send()

        for d in range(1, row_len):
            row_copy(lax.rem(my_x + d, row_len), mb).wait_send()
        for dest in range(1, col_len):

            @pl.when(dest > my_y)
            def _():
                col_copy(dest, mb).wait_send()

    for d in range(1, size):
        square_copy(d).wait_send()

    @pl.when(seq < seq_len - 1)
    def _():
        doc_copy.wait_send()


def per_device(
    stream,
    segment_ids,
    norm_gain,
    in_weight,
    bc_weight,
    dt_weight,
    dt_bias,
    decay_rate,
    conv_inner,
    conv_state,
    skip_gain,
    inner_gain,
    out_weight,
):
    size = lax.axis_size("mp")
    seq_len = lax.axis_size("seq")
    row_len = math.isqrt(seq_len)
    col_len = seq_len // row_len
    local = stream.shape[-1]
    depth = in_weight.shape[1]
    width = in_weight.shape[-1]
    heads = width // HDIM
    states = bc_weight.shape[-1]
    far = size // 2
    near = max(size - 1 - far, 1)
    whole = pl.BlockSpec(memory_space=pltpu.VMEM)
    apart = pl.BlockSpec(memory_space=pl.ANY)
    part = (MB, TOK, local)
    dma = pltpu.SemaphoreType.DMA
    scratch = [
        pltpu.VMEM(part, BF16),
        pltpu.VMEM((far, *part), BF16),
        pltpu.VMEM((near, *part), BF16),
        pltpu.VMEM((depth, 2 * width), BF16),
        pltpu.VMEM((depth, states), BF16),
        pltpu.VMEM((depth, heads), BF16),
        pltpu.VMEM(out_weight.shape[1:], BF16),
        pltpu.VMEM((size, local), F32),
        pltpu.VMEM((MB, TOK, 2 * width), F32),
        pltpu.VMEM((MB, TOK, states), F32),
        pltpu.VMEM((MB, TOK, heads), F32),
        pltpu.VMEM((MB, TOK, 1), F32),
        pltpu.VMEM((MB, TOK, width + states), BF16),
        pltpu.VMEM((MB, LAG, width + states), BF16),
        pltpu.VMEM((MB, TOK), jnp.int32),
        pltpu.VMEM((LAG + TOK, width + states), F32),
        pltpu.VMEM((LAG + TOK, TOK), F32),
        pltpu.VMEM((MB, TOK, width), BF16),
        pltpu.VMEM((MB, TOK, STATE), BF16),
        pltpu.VMEM((MB, TOK, heads), F32),
        pltpu.VMEM((MB, TOK, TOK), F32),
        pltpu.VMEM((MB, TOK, TOK), F32),
        pltpu.VMEM((MB, TOK, width), F32),
        pltpu.VMEM((MB, TOK, width), F32),
        pltpu.VMEM((row_len, MB, PACK, width), BF16),
        pltpu.VMEM((col_len, MB, PACK, width), BF16),
        pltpu.VMEM((MB, PACK, width), BF16),
        pltpu.VMEM((STATE, width), F32),
        pltpu.VMEM((1, width), F32),
        pltpu.VMEM((MB, STATE, width), F32),
        pltpu.VMEM((MB, 1, width), F32),
        pltpu.VMEM((MB, TOK, width), BF16),
        pltpu.VMEM((8, TOK), F32),
        pltpu.VMEM((size, 8, TOK), F32),
        pltpu.VMEM((size, *part), BF16),
        pltpu.VMEM((far, *part), BF16),
        pltpu.VMEM((near, *part), BF16),
        pltpu.VMEM((far, *part), BF16),
        pltpu.VMEM((near, *part), BF16),
        dma((size, 3)),
        dma((2,)),
        dma((far, MB)),
        dma((far, MB)),
        dma((near, MB)),
        dma((near, MB)),
        dma((MB,)),
        dma((MB,)),
        dma,
        dma,
        dma((row_len, MB)),
        dma((row_len, MB)),
        dma((col_len, MB)),
        dma((col_len, MB)),
        dma((size,)),
        dma((size,)),
        dma((far, MB)),
        dma((far, MB)),
        dma((near, MB)),
        dma((near, MB)),
        dma((MB,)),
        dma((MB,)),
    ]
    return pl.pallas_call(
        functools.partial(kernel, size, row_len, seq_len),
        out_shape=jax.ShapeDtypeStruct((1, *part), BF16),
        in_specs=[
            apart,
            whole,
            whole,
            apart,
            apart,
            apart,
            whole,
            whole,
            whole,
            whole,
            whole,
            whole,
            apart,
        ],
        out_specs=whole,
        scratch_shapes=scratch,
        compiler_params=pltpu.CompilerParams(
            collective_id=0, has_side_effects=True, vmem_limit_bytes=60 << 20
        ),
        name="mixer_layers",
    )(
        stream,
        segment_ids,
        norm_gain,
        in_weight[0].reshape(depth, 2 * width),
        bc_weight[0],
        dt_weight[0],
        dt_bias,
        decay_rate,
        conv_inner,
        conv_state,
        skip_gain,
        inner_gain,
        out_weight[0],
    )


def solution(mesh):
    placed = (
        P(None, "seq", "mp"),
        P(None, "seq"),
        P("section", None),
        P("section", None, None, "mp"),
        P("section", None, None),
        P("section", None, "mp"),
        P("section", "mp"),
        P("section", "mp"),
        P("section", None, "mp"),
        P("section", None, None),
        P("section", "mp"),
        P("section", "mp"),
        P("section", "mp", None),
    )
    return jax.shard_map(
        per_device,
        mesh=mesh,
        in_specs=placed,
        out_specs=P("section", None, "seq", "mp"),
        check_vma=False,
    )
```

profile of v0, /device:TPU:25, one launch (start us, length us, event | category | flops | bytes accessed | tf_op | source)
XLA Modules:
  0.0 121.3 jit_solution(314733344698474662)
XLA Ops:
  0.0 1.8 %copy.15.stream = bf16[2,128,448]{2,1,0:T(8,128)(2,1)} copy(bf16[2,128,448]{1,2,0:T(8,128)(2,1)} %param.13) | data formatting | bytes 458752 | tf_op args[0]
  1.8 2.0 %copy.14 = bf16[1,3584,8]{2,1,0:T(8,128)(2,1)} copy(bf16[1,3584,8]{1,2,0:T(8,128)(2,1)} %param.18) | data formatting | bytes 114688 | tf_op args[5]
  3.9 8.4 %copy.17 = bf16[448,8,2,512]{3,1,2,0:T(8,128)(2,1)} copy(bf16[448,8,2,512]{3,2,1,0:T(2,128)(2,1)} %bitcast.7) | data formatting | bytes 14680064
  12.3 107.3 %mixer_layers.1 = bf16[1,2,128,448]{3,2,1,0:T(8,128)(2,1)} custom-call(bf16[2,128,448]{2,1,0:T(8,128)(2,1)} %copy.15.stream, s32[2,128]{1,0:T(2,128)} %seg.1, bf16[1,3584]{1,0:T(2,128)(2,1)} %norm_gain.1, bf16[3584,1024]{1,0:T(8,128)(2,1)} %bitcast.6, bf16[3584,128]{1,0:T(8,128)(2,1)} %bitcast.10, bf16[3584,8]{1,0:T(8,128)(2,1)} %bitcast.9, f32[1,8]{1,0:T(1,128)} %dt_bias.1, ...), custom_call_target="tpu_custom_call" | custom-call | tf_op jit(solution)/shard_map/mixer_layers/pallas_call | solution.py:708
  119.5 1.8 %copy.16 = bf16[1,2,128,448]{2,3,1,0:T(8,128)(2,1)} copy(bf16[1,2,128,448]{3,2,1,0:T(8,128)(2,1)} %mixer_layers.1) | data formatting | bytes 458752 | tf_op jit(solution)/shard_map/mixer_layers/pallas_call | solution.py:708
where the time goes:
time: 122 us; the launch traced here: 121 us
  Pallas kernels  107 us (88%)
  local copies, waits for them, and re-layouts  14 us (11%)
    pallas_call x1, Pallas kernels, per_device(): pl.pallas_call(functools.partial(kernel, size, row_len, seq_len), out_sha...  107 us
    unnamed x3, local copies, waits for them, and re-layouts  12.3 us

commit v1 on v0

--- a/solution.py
+++ b/solution.py
@@ -18,6 +18,7 @@
 MB = 2
 LAG = 16
 PACK = STATE + 16
+SUB = 2
 
 
 def spread(row):
@@ -49,15 +50,19 @@
     xin,
     gr,
     gl,
+    wraw,
     wi,
     wb,
     wd,
     wo,
+    wot,
     gains,
     acc,
     accs,
     accd,
     ss,
+    rows_scale,
+    cols_scale,
     jn,
     halo,
     prev,
@@ -108,8 +113,10 @@
     sx_s,
     sx_r,
 ):
-    local = stream.shape[-1]
+    local = stream.shape[1]
+    piece = local // SUB
     width = wo.shape[0]
+    heads = width // HDIM
     state_at = width
     col_len = seq_len // row_len
     far = size // 2
@@ -150,9 +157,8 @@
         rows = rows_of(rel)
         k = slot_of[rel]
         return [
-            pltpu.make_async_copy(w_in.at[rows], wi.at[rows], w_sem.at[k, 0]),
+            pltpu.make_async_copy(w_in.at[rows], wraw.at[rows], w_sem.at[k, 0]),
             pltpu.make_async_copy(w_bc.at[rows], wb.at[rows], w_sem.at[k, 1]),
-            pltpu.make_async_copy(w_dt.at[rows], wd.at[rows], w_sem.at[k, 2]),
         ]
 
     out_copy = pltpu.make_async_copy(w_out, wo, x_sem.at[1])
@@ -194,7 +200,10 @@
         halo[...] = jnp.zeros_like(halo)
 
     for j in range(size):
-        gains[j : j + 1, :] = norm_gain[0:1, j * local : (j + 1) * local].astype(F32)
+        lanes = slice(j * local, (j + 1) * local)
+        gain = norm_gain[0:1, lanes].astype(F32)
+        gains[j : j + 1, :] = gain
+        wd[j] = (w_dt[:, lanes].astype(F32) * gain).astype(BF16)
 
     pass_on = [
         remote(out.at[0, mb], xin.at[mb], sx_s.at[mb], sx_r.at[mb], {"section": 1 - section})
@@ -205,36 +214,62 @@
     def _():
         first_copy.wait()
 
-    def gather_copy(side, step, mb):
+    def hops(side, mb):
+        return far if (side > 0) == (mb == 0) else near
+
+    def cut(part):
+        return pl.ds(part * piece, piece)
+
+    def gather_copy(side, step, mb, part):
         bank, send, recv = (gr, agr_s, agr_r) if side > 0 else (gl, agl_s, agl_r)
-        src = xin.at[mb] if step == 0 else bank.at[step - 1, mb]
+        src = xin.at[mb, cut(part)] if step == 0 else bank.at[step - 1, mb, cut(part)]
         return remote(
-            src, bank.at[step, mb], send.at[step, mb], recv.at[step, mb], to_mp(side)
-        )
-
-    def project(values, rel, first):
+            src,
+            bank.at[step, mb, cut(part)],
+            send.at[step, mb, part],
+            recv.at[step, mb, part],
+            to_mp(side),
+        )
+
+    def project(blocks, rel, first):
         for copy in weight_copies(rel):
             copy.wait()
         owner = at_mp(rel)
         rows = rows_of(rel)
-        wide = values.reshape(MB * TOK, local).astype(F32)
-        square = jnp.sum(wide * wide, axis=1, keepdims=True).reshape(MB, TOK, 1)
-        scaled = (wide * gains[pl.ds(owner, 1), :]).astype(BF16)
+        halves = pltpu.einshape("ksl->skl", wraw[rows])
+        wi[:, :width] = halves[0]
+        wi[:, width:] = halves[1]
+        gain = gains[pl.ds(owner, 1), :]
+        lhs = []
+        for mb, block in enumerate(blocks):
+            wide = block.astype(F32)
+            square = jnp.sum(wide * wide, axis=0, keepdims=True)
+            step_raw = jnp.dot(wd[owner], block, preferred_element_type=F32)
+            if first:
+                ss[mb : mb + 1] = square
+                accd[mb] = step_raw
+            else:
+                ss[mb : mb + 1] += square
+                accd[mb] += step_raw
+            lhs.append((block.T.astype(F32) * gain).astype(BF16))
+        scaled = jnp.concatenate(lhs, axis=0)
         block = 256
-        pieces = [(acc, wi, n * block, block) for n in range(2 * width // block)]
-        pieces += [(accs, wb, 0, wb.shape[1]), (accd, wd, 0, wd.shape[1])]
-        for total, weight, start, count in pieces:
-            term = jnp.dot(
-                scaled, weight[rows, start : start + count], preferred_element_type=F32
-            ).reshape(MB, TOK, count)
+        pieces = [
+            (acc, n * block, wi[:, n * block : (n + 1) * block])
+            for n in range(2 * width // block)
+        ]
+        pieces += [(accs, 0, wb[rows, :])]
+        for total, start, weight in pieces:
+            count = weight.shape[1]
+            term = jnp.dot(scaled, weight, preferred_element_type=F32).reshape(MB, TOK, count)
             if first:
                 total[:, :, start : start + count] = term
             else:
                 total[:, :, start : start + count] += term
-        if first:
-            ss[...] = square
-        else:
-            ss[...] += square
+
+    def turn(first, count):
+        for c in range(first, first + count):
+            wot[c * TOK : (c + 1) * TOK, :] = wo[:, c * TOK : (c + 1) * TOK].T
 
     for mb in range(MB):
 
@@ -242,21 +277,27 @@
         def _():
             pass_on[mb].wait_recv()
 
-        gather_copy(1, 0, mb).start()
-        gather_copy(-1, 0, mb).start()
-    project(xin[...], 0, True)
+        for part in range(SUB):
+            for side in (1, -1):
+                if hops(side, mb) > 0:
+                    gather_copy(side, 0, mb, part).start()
+    project([xin[mb] for mb in range(MB)], 0, True)
+    out_copy.wait()
+    turns = size * local // TOK // far
     for step in range(far):
-        for mb in range(MB):
-            gather_copy(1, step, mb).wait_recv()
-            if step + 1 < far:
-                gather_copy(1, step + 1, mb).start()
-            if step < near:
-                gather_copy(-1, step, mb).wait_recv()
-                if step + 1 < near:
-                    gather_copy(-1, step + 1, mb).start()
-        project(gr[step], -1 - step, False)
+        for part in range(SUB):
+            for mb in range(MB):
+                for side in (1, -1):
+                    if step < hops(side, mb):
+                        gather_copy(side, step, mb, part).wait_recv()
+                    if step + 1 < hops(side, mb):
+                        gather_copy(side, step + 1, mb, part).start()
         if step < near:
-            project(gl[step], 1 + step, False)
+            project([gr[step, mb] for mb in range(MB)], -1 - step, False)
+            project([gl[step, mb] for mb in range(MB)], 1 + step, False)
+        else:
+            project([gr[step, 0], gl[step, 1]], -1 - step, False)
+        turn(step * turns, turns)
 
     def halo_copy(mb):
         return remote(
@@ -268,8 +309,10 @@
         )
 
     def join(mb, carry):
-        scale = lax.rsqrt(ss[mb] / (size * local) + EPS)
-        ss[mb] = scale
+        row = lax.rsqrt(ss[pl.ds(mb, 1), :] / (size * local) + EPS)
+        scale = spread(row).T[:, 0:1]
+        rows_scale[pl.ds(mb, 1), :] = row
+        cols_scale[mb] = scale
         jn[mb, :, :width] = (acc[mb, :, :width] * scale).astype(BF16)
         jn[mb, :, width:] = (accs[mb] * scale).astype(BF16)
 
@@ -281,7 +324,6 @@
 
     lax.fori_loop(0, MB, join, 0)
 
-    heads = width // HDIM
     spread_heads = (
         lax.broadcasted_iota(jnp.int32, (heads, width), 1) // HDIM
         == lax.broadcasted_iota(jnp.int32, (heads, width), 0)
@@ -335,6 +377,16 @@
             py_r.at[source, mb],
             {"seq": source * row_len + my_x},
         )
+
+    same = lax.broadcasted_iota(jnp.int32, (heads, heads), 0) == lax.broadcasted_iota(
+        jnp.int32, (heads, heads), 1
+    )
+
+    def stand(row):
+        return jnp.sum(jnp.where(same, row, 0.0), axis=1, keepdims=True)
+
+    bias = stand(dt_bias[...])
+    rate = stand(decay_rate[...])
 
     @pl.when(seq > 0)
     def _():
@@ -350,18 +402,25 @@
         prior = old_col[TOK - 1 : TOK, 0:1]
         last = own_col[TOK - 1 : TOK, 0:1]
 
-        scale = ss[mb]
-        raw = accd[mb] * scale + dt_bias[...]
-        steps_dt = jnp.maximum(raw, 0.0) + jnp.log1p(jnp.exp(-jnp.abs(raw)))
+        raw = accd[mb] * rows_scale[pl.ds(mb, 1), :] + bias
+        steps_flat = jnp.maximum(raw, 0.0) + jnp.log1p(jnp.exp(-jnp.abs(raw)))
         places_t = lax.broadcasted_iota(jnp.int32, (TOK, TOK), 0)
         places_s = lax.broadcasted_iota(jnp.int32, (TOK, TOK), 1)
         lower = places_t >= places_s
-        cumlog = jnp.dot(
-            lower.astype(F32),
-            -steps_dt * decay_rate[...],
+        cum_flat = jnp.dot(
+            -steps_flat * rate,
+            (places_t <= places_s).astype(F32),
             precision=HIGH,
             preferred_element_type=F32,
         )
+        flat = jnp.concatenate(
+            [cum_flat, steps_flat, jnp.zeros((TOK - 2 * heads, TOK), F32)], axis=0
+        )
+        flats[mb] = flat
+        stood = flat.T
+        cumlog = stood[:, 0:heads]
+        steps_dt = stood[:, heads : 2 * heads]
+        cums[mb] = cumlog
         tail = jnp.where(doc == last, jnp.exp(cumlog[TOK - 1 : TOK] - cumlog), 0.0) * steps_dt
         carry_in = jnp.where(doc == prior, jnp.exp(cumlog), 0.0)
         tail_wide = expand(tail)
@@ -396,11 +455,6 @@
         b_cols = both.T[0:STATE].astype(BF16)
         c_rows = pltpu.roll(both, STATE, axis=1)[:, 0:STATE].astype(BF16)
         cs[mb] = c_rows
-        cums[mb] = cumlog
-        flats[mb] = jnp.concatenate(
-            [cumlog, steps_dt, jnp.zeros((TOK, TOK - 2 * heads), F32)], axis=1
-        ).T
-
         for j, part in enumerate(inputs):
             lanes = slice(j * TOK, (j + 1) * TOK)
             us[mb, :, lanes] = part
@@ -497,7 +551,7 @@
         entering = (pre_a[mb] * cur_s[...] + pre_s[mb]).astype(BF16)
         from_state = jnp.dot(cs[mb], entering, preferred_element_type=F32)
         results = lo[mb] + ce[mb] * from_state
-        gate = acc[mb, :, width:] * ss[mb]
+        gate = acc[mb, :, width:] * cols_scale[mb]
         gated = results * (gate * sigmoid(gate))
         square = jnp.sum(gated * gated, axis=1, keepdims=True)
         sq[pl.ds(mb, 1), :] = jnp.broadcast_to(square, (TOK, TOK)).T[0:1]
@@ -516,47 +570,60 @@
     for d in range(1, size):
         square_copy(d).start()
 
-    out_copy.wait()
-    pairs = size // 2
-    my_pair = lax.div(me, 2)
-    for i in range(pairs):
-        pair = lax.rem(my_pair + (pairs // 2 + i), pairs)
-        start = pl.multiple_of(pair * (2 * local), TOK)
-        term = jnp.dot(
-            gb[...].reshape(MB * TOK, width),
-            wo[:, pl.ds(start, 2 * local)],
+    gated_all = gb[...].reshape(MB * TOK, width)
+
+    def produce(rel):
+        term = lax.dot_general(
+            wot[rows_of(rel), :],
+            gated_all,
+            (((1,), (1,)), ((), ())),
             preferred_element_type=F32,
         ).astype(BF16)
-        for half in range(2):
-            upd[2 * pair + half] = term[:, half * local : (half + 1) * local].reshape(
-                MB, TOK, local
-            )
-
-    def scatter_copy(side, step, mb):
+        for mb in range(MB):
+            upd[at_mp(rel), mb] = term[:, mb * TOK : (mb + 1) * TOK]
+
+    def scatter_copy(side, step, mb, part):
         if side > 0:
-            bank, mine, send, recv, rel = rr, sr, rsr_s, rsr_r, far
+            bank, mine, send, recv = rr, sr, rsr_s, rsr_r
         else:
-            bank, mine, send, recv, rel = rl, sl, rsl_s, rsl_r, -near
+            bank, mine, send, recv = rl, sl, rsl_s, rsl_r
+        rel = side * (hops(side, mb) - step)
         src = upd.at[at_mp(rel), mb] if step == 0 else mine.at[step - 1, mb]
         return remote(
-            src, bank.at[step, mb], send.at[step, mb], recv.at[step, mb], to_mp(side)
-        )
-
-    def add_term(bank, step, mb, rel):
-        return bank[step, mb].astype(F32) + upd[at_mp(rel), mb].astype(F32)
-
-    for mb in range(MB):
-        scatter_copy(1, 0, mb).start()
-        scatter_copy(-1, 0, mb).start()
+            src.at[cut(part)],
+            bank.at[step, mb, cut(part)],
+            send.at[step, mb, part],
+            recv.at[step, mb, part],
+            to_mp(side),
+        )
+
+    def add_term(bank, step, mb, part, rel):
+        rows = cut(part)
+        return bank[step, mb, rows].astype(F32) + upd[at_mp(rel), mb, rows].astype(F32)
+
+    produce(far)
+    for part in range(SUB):
+        for mb in range(MB):
+            scatter_copy(1 if mb == 0 else -1, 0, mb, part).start()
+    for rel in (near, -near) if near > 0 else ():
+        produce(rel)
+        for part in range(SUB):
+            scatter_copy(1 if rel > 0 else -1, 0, 1 if rel > 0 else 0, part).start()
+    for rel in range(near - 1, 0, -1):
+        produce(rel)
+        produce(-rel)
+    produce(0)
     for step in range(1, far):
-        for mb in range(MB):
-            scatter_copy(1, step - 1, mb).wait_recv()
-            sr[step - 1, mb] = add_term(rr, step - 1, mb, far - step).astype(BF16)
-            scatter_copy(1, step, mb).start()
-            if step < near:
-                scatter_copy(-1, step - 1, mb).wait_recv()
-                sl[step - 1, mb] = add_term(rl, step - 1, mb, step - near).astype(BF16)
-                scatter_copy(-1, step, mb).start()
+        for part in range(SUB):
+            for mb in range(MB):
+                for side, bank, mine in ((1, rr, sr), (-1, rl, sl)):
+                    if step < hops(side, mb):
+                        scatter_copy(side, step - 1, mb, part).wait_recv()
+                        rel = side * (hops(side, mb) - step)
+                        mine[step - 1, mb, cut(part)] = add_term(
+                            bank, step - 1, mb, part, rel
+                        ).astype(BF16)
+                        scatter_copy(side, step, mb, part).start()
 
     for d in range(1, size):
         square_arrival(d).wait_recv()
@@ -566,14 +633,19 @@
         squares = squares + sqr[j]
 
     for mb in range(MB):
-        if near > 0:
-            scatter_copy(-1, near - 1, mb).wait_recv()
-        scatter_copy(1, far - 1, mb).wait_recv()
-        total = add_term(rr, far - 1, mb, 0)
-        if near > 0:
-            total = total + rl[near - 1, mb].astype(F32)
-        mean = spread(squares[mb : mb + 1]).T[:, 0:1] / (size * width)
-        out[0, mb] = (xin[mb].astype(F32) + total * lax.rsqrt(mean + EPS)).astype(BF16)
+        factor = lax.rsqrt(squares[mb : mb + 1] / (size * width) + EPS)
+        main, other = (1, -1) if mb == 0 else (-1, 1)
+        first_bank, last_bank = (rl, rr) if mb == 0 else (rr, rl)
+        for part in range(SUB):
+            if near > 0:
+                scatter_copy(other, near - 1, mb, part).wait_recv()
+            scatter_copy(main, far - 1, mb, part).wait_recv()
+            total = add_term(last_bank, far - 1, mb, part, 0)
+            if near > 0:
+                total = total + first_bank[near - 1, mb, cut(part)].astype(F32)
+            out[0, mb, cut(part)] = (
+                xin[mb, cut(part)].astype(F32) + total * factor
+            ).astype(BF16)
 
         @pl.when(section == 0)
         def _():
@@ -585,12 +657,11 @@
         def _():
             pass_on[mb].wait_send()
 
-        for step in range(far):
-            gather_copy(1, step, mb).wait_send()
-            scatter_copy(1, step, mb).wait_send()
-        for step in range(near):
-            gather_copy(-1, step, mb).wait_send()
-            scatter_copy(-1, step, mb).wait_send()
+        for part in range(SUB):
+            for side in (1, -1):
+                for step in range(hops(side, mb)):
+                    gather_copy(side, step, mb, part).wait_send()
+                    scatter_copy(side, step, mb, part).wait_send()
 
         @pl.when(seq < seq_len - 1)
         def _():
@@ -637,23 +708,26 @@
     heads = width // HDIM
     states = bc_weight.shape[-1]
     far = size // 2
-    near = max(size - 1 - far, 1)
     whole = pl.BlockSpec(memory_space=pltpu.VMEM)
     apart = pl.BlockSpec(memory_space=pl.ANY)
-    part = (MB, TOK, local)
+    part = (MB, local, TOK)
     dma = pltpu.SemaphoreType.DMA
     scratch = [
         pltpu.VMEM(part, BF16),
         pltpu.VMEM((far, *part), BF16),
-        pltpu.VMEM((near, *part), BF16),
-        pltpu.VMEM((depth, 2 * width), BF16),
+        pltpu.VMEM((far, *part), BF16),
+        pltpu.VMEM((depth, 2, width), BF16),
+        pltpu.VMEM((local, 2 * width), BF16),
         pltpu.VMEM((depth, states), BF16),
-        pltpu.VMEM((depth, heads), BF16),
+        pltpu.VMEM((size, heads, local), BF16),
         pltpu.VMEM(out_weight.shape[1:], BF16),
+        pltpu.VMEM((depth, width), BF16),
         pltpu.VMEM((size, local), F32),
         pltpu.VMEM((MB, TOK, 2 * width), F32),
         pltpu.VMEM((MB, TOK, states), F32),
-        pltpu.VMEM((MB, TOK, heads), F32),
+        pltpu.VMEM((MB, heads, TOK), F32),
+        pltpu.VMEM((MB, TOK), F32),
+        pltpu.VMEM((MB, TOK), F32),
         pltpu.VMEM((MB, TOK, 1), F32),
         pltpu.VMEM((MB, TOK, width + states), BF16),
         pltpu.VMEM((MB, LAG, width + states), BF16),
@@ -679,15 +753,15 @@
         pltpu.VMEM((size, 8, TOK), F32),
         pltpu.VMEM((size, *part), BF16),
         pltpu.VMEM((far, *part), BF16),
-        pltpu.VMEM((near, *part), BF16),
         pltpu.VMEM((far, *part), BF16),
-        pltpu.VMEM((near, *part), BF16),
-        dma((size, 3)),
+        pltpu.VMEM((far, *part), BF16),
+        pltpu.VMEM((far, *part), BF16),
+        dma((size, 2)),
         dma((2,)),
-        dma((far, MB)),
-        dma((far, MB)),
-        dma((near, MB)),
-        dma((near, MB)),
+        dma((far, MB, SUB)),
+        dma((far, MB, SUB)),
+        dma((far, MB, SUB)),
+        dma((far, MB, SUB)),
         dma((MB,)),
         dma((MB,)),
         dma,
@@ -698,14 +772,14 @@
         dma((col_len, MB)),
         dma((size,)),
         dma((size,)),
-        dma((far, MB)),
-        dma((far, MB)),
-        dma((near, MB)),
-        dma((near, MB)),
+        dma((far, MB, SUB)),
+        dma((far, MB, SUB)),
+        dma((far, MB, SUB)),
+        dma((far, MB, SUB)),
         dma((MB,)),
         dma((MB,)),
     ]
-    return pl.pallas_call(
+    result = pl.pallas_call(
         functools.partial(kernel, size, row_len, seq_len),
         out_shape=jax.ShapeDtypeStruct((1, *part), BF16),
         in_specs=[
@@ -714,7 +788,7 @@
             whole,
             apart,
             apart,
-            apart,
+            whole,
             whole,
             whole,
             whole,
@@ -730,12 +804,12 @@
         ),
         name="mixer_layers",
     )(
-        stream,
+        stream.transpose(0, 2, 1),
         segment_ids,
         norm_gain,
-        in_weight[0].reshape(depth, 2 * width),
+        in_weight[0],
         bc_weight[0],
-        dt_weight[0],
+        dt_weight[0].T,
         dt_bias,
         decay_rate,
         conv_inner,
@@ -744,6 +818,7 @@
         inner_gain,
         out_weight[0],
     )
+    return result.transpose(0, 1, 3, 2)
 
 
 def solution(mesh):

time: 122 us -> 104 us (0.85)
  local copies, waits for them, and re-layouts: 14 us -> 1.64 us
  Pallas kernels: 107 us -> 102 us
    unnamed x3 -> x1, local copies, waits for them, and re-layouts: 12.3 us -> 1.64 us
    pallas_call x1, Pallas kernels: 107 us -> 102 us  [per_device(): pl.pallas_call(functools.partial(kernel, size, row_len, seq_len), out_sha...]
    pallas_call x1 -> x0, local copies, waits for them, and re-layouts: 1.78 us -> none  [per_device(): pl.pallas_call(functools.partial(kernel, size, row_len, seq_len), out_sha...]
where the time goes in v1:
time: 104 us; the launch traced here: 103 us
  Pallas kernels  102 us (98%)
  local copies, waits for them, and re-layouts  1.64 us (2%)
    pallas_call x1, Pallas kernels, per_device(): pl.pallas_call(functools.partial(kernel, size, row_len, seq_len), out_sha...  102 us

profile of v1, /device:TPU:25, one launch (start us, length us, event | category | flops | bytes accessed | tf_op | source)
XLA Modules:
  0.0 103.4 jit_solution(6586418613877634049)
XLA Ops:
  0.0 101.8 %mixer_layers.1 = bf16[1,2,448,128]{3,2,1,0:T(8,128)(2,1)} custom-call(bf16[2,448,128]{2,1,0:T(8,128)(2,1)} %bitcast.12, s32[2,128]{1,0:T(2,128)} %seg.1, bf16[1,3584]{1,0:T(2,128)(2,1)} %norm_gain.1, bf16[3584,2,512]{2,1,0:T(2,128)(2,1)} %bitcast.8, bf16[3584,128]{1,0:T(8,128)(2,1)} %bitcast.10, bf16[8,3584]{1,0:T(8,128)(2,1)} %bitcast.13, f32[1,8]{1,0:T(1,128)} %dt_bias.1, ...), custom_call_target="tpu_custom_call" | custom-call | tf_op jit(solution)/shard_map/mixer_layers/pallas_call | solution.py:782
  101.8 1.6 %copy.15 = bf16[1,2,128,448]{2,3,1,0:T(8,128)(2,1)} copy(bf16[1,2,128,448]{2,3,1,0:T(8,128)(2,1)} %bitcast.11) | data formatting | bytes 458752
